TPU v7x, 512 devices: a whole 4x8x8 slice. The times are simulated.
512 devices in a mesh: ctx: 128 (over y, x_hi, z), head: 4 (over x_lo, core).
Axes of the slice: x: 4 (x_hi: 2, x_lo: 2; x = x_hi * 2 + x_lo), y: 8, z: 8, core: 2. Of those that a mesh axis runs over, the one named last changes fastest.
Arguments:
- text_query: bfloat16 [16384, 2560], P('ctx', 'head')
- grad_out: bfloat16 [16384, 2560], P('ctx', 'head'), may hold values from -6 to 6
- frame_kv: bfloat16 [2, 65536, 2560], P(None, 'ctx', 'head')
- sink_logit: float32 [20], P('head'), may hold values from 1 to 6
- pairing: int32 [128], replicated, may hold values from 0 to 127, each once
- block_mask: int32 [128, 4], P('ctx'), may hold values from 0 to 1
- text_seg: int32 [16384], P('ctx'), may hold values from 0 to 3, as said below
- frame_seg: int32 [65536], P('ctx'), may hold values from 0 to 3, as said below
Outputs:
- grad_query: bfloat16 [16384, 2560], P('ctx', 'head')
- grad_kv: bfloat16 [2, 65536, 2560], P(None, ('ctx', 'head'))
Inputs may be any that keep to these rules, and one draw needn't show every extreme that they name: pairing is a permutation of the ctx indices. `text_seg`: within the 128 text tokens of each ctx index the ids do not fall and each of the 4 ids appears. `frame_seg`: within the 512 frames of each ctx index the ids do not fall and each of the 4 ids appears.
All inputs are finite; a program needn't handle non-finite values.
Results may differ from a plain program's by a relative error of at most 0.0081.
Values may be sent and summed in bfloat16 or wider, within the bound.
A program may use at most 64 MiB of HBM per device.

v0:
```python
import jax
import jax.numpy as jnp
from jax import lax
from jax.sharding import PartitionSpec as P

DH = 128
BLOCK = 128


def attend(query_rows, grad_rows, key_rows, value_rows, row_mask, text_ids, frame_ids, sink_logit):
    score_scale = DH ** (-0.5)
    text_rows = query_rows.shape[0]
    frame_rows = key_rows.shape[0]
    head_count = query_rows.shape[1] // DH
    q_heads = query_rows.reshape(text_rows, head_count, DH)
    g_heads = grad_rows.reshape(text_rows, head_count, DH)
    k_heads = key_rows.reshape(frame_rows, head_count, DH)
    v_heads = value_rows.reshape(frame_rows, head_count, DH)
    allowed = (jnp.repeat(row_mask, BLOCK, axis=1) == 1) & (text_ids[:, None] == frame_ids[None, :])
    scores = (
        jnp.einsum("the,fhe->htf", q_heads, k_heads, preferred_element_type=jnp.float32)
        * score_scale
    )
    masked = jnp.where(allowed[None], scores, -1e30)
    row_top = jnp.maximum(sink_logit[:, None], jnp.max(masked, axis=2))
    exp_terms = jnp.where(allowed[None], jnp.exp(masked - row_top[:, :, None]), 0.0)
    row_total = jnp.exp(sink_logit[:, None] - row_top) + jnp.sum(exp_terms, axis=2)
    attention = exp_terms / row_total[:, :, None]
    attention_low = attention.astype(jnp.bfloat16)
    output = jnp.einsum("htf,fhe->the", attention_low, v_heads, preferred_element_type=jnp.float32)
    grad_attention = jnp.einsum(
        "the,fhe->htf", g_heads, v_heads, preferred_element_type=jnp.float32
    )
    row_delta = jnp.sum(g_heads.astype(jnp.float32) * output, axis=2)
    grad_scores = (attention * (grad_attention - row_delta.T[:, :, None])).astype(jnp.bfloat16)
    grad_query = (
        jnp.einsum("htf,fhe->the", grad_scores, k_heads, preferred_element_type=jnp.float32)
        * score_scale
    )
    grad_keys = (
        jnp.einsum("htf,the->fhe", grad_scores, q_heads, preferred_element_type=jnp.float32)
        * score_scale
    )
    grad_values = jnp.einsum(
        "htf,the->fhe", attention_low, g_heads, preferred_element_type=jnp.float32
    )
    grad_pair = jnp.stack([grad_keys.reshape(frame_rows, -1), grad_values.reshape(frame_rows, -1)])
    return (grad_query.reshape(text_rows, -1).astype(jnp.bfloat16), grad_pair.astype(jnp.bfloat16))


def shards(text_query, grad_out, frame_kv, sink_logit, pairing, block_mask, text_seg, frame_seg):
    owners = lax.axis_size("ctx")
    text_rows = text_query.shape[0]
    feature_width = text_query.shape[1]
    frame_blocks = block_mask.shape[1]
    indices = jnp.arange(owners, dtype=jnp.int32)
    inverse = jnp.sum(jnp.where(pairing[None, :] == indices[:, None], indices[None, :], 0), axis=1)
    row_mask = jnp.repeat(block_mask, BLOCK, axis=0)
    stacked = jnp.stack([text_query, grad_out]).reshape(
        2, owners, text_rows // owners, feature_width
    )
    text_tags = jnp.concatenate([text_seg[:, None], row_mask], axis=1).astype(jnp.bfloat16)
    text_tags = text_tags.reshape(1, owners, text_rows // owners, frame_blocks + 1)
    first_text, first_tags = (
        lax.all_to_all(stacked, "ctx", split_axis=1, concat_axis=1, tiled=True),
        lax.all_to_all(text_tags, "ctx", split_axis=1, concat_axis=1, tiled=True),
    )
    second_text, second_tags = (
        lax.all_to_all(
            jnp.take(first_text, inverse, axis=1), "ctx", split_axis=1, concat_axis=1, tiled=True
        ),
        lax.all_to_all(
            jnp.take(first_tags, inverse, axis=1), "ctx", split_axis=1, concat_axis=1, tiled=True
        ),
    )
    visiting = second_text.reshape(2, text_rows, feature_width)
    visiting_tags = second_tags.reshape(text_rows, frame_blocks + 1).astype(jnp.int32)
    grad_visit, home_adjoint = attend(
        visiting[0],
        visiting[1],
        frame_kv[0],
        frame_kv[1],
        visiting_tags[:, 1:],
        visiting_tags[:, 0],
        frame_seg,
        sink_logit,
    )
    returning = lax.all_to_all(
        grad_visit.reshape(1, owners, text_rows // owners, feature_width),
        "ctx",
        split_axis=1,
        concat_axis=1,
        tiled=True,
    )
    grad_query = lax.all_to_all(
        jnp.take(returning, pairing, axis=1), "ctx", split_axis=1, concat_axis=1, tiled=True
    ).reshape(text_rows, feature_width)
    grad_kv = lax.all_to_all(home_adjoint, "head", split_axis=1, concat_axis=2, tiled=True)
    return (grad_query, grad_kv)


def solution(mesh):
    in_specs = (
        P("ctx", "head"),
        P("ctx", "head"),
        P(None, "ctx", "head"),
        P("head"),
        P(),
        P("ctx", None),
        P("ctx"),
        P("ctx"),
    )
    out_specs = (P("ctx", "head"), P(None, ("ctx", "head"), None))
    return jax.shard_map(shards, mesh=mesh, in_specs=in_specs, out_specs=out_specs, check_vma=False)
```

profile of v0, /device:TPU:1, one launch (start us, length us, event | category | flops | bytes accessed | tf_op | source)
XLA Modules:
  0.0 181.7 jit_solution(7947610529917276390)
XLA Ops:
  0.7 0.8 convert_bitcast_fusion
  1.4 0.7 convert_bitcast_fusion.1
  2.1 0.1 pad.5.clone
  2.1 0.1 pad_maximum_fusion.1
  2.2 0.8 copy.78
  3.0 20.8 %all-to-all-start = ((bf16[1,128,1,5]{3,2,0,1:T(2,128)(2,1)}), bf16[1,128,1,5]{3,2,0,1:T(2,128)(2,1)S(1)}, u32[]{:S(2)}, u32[]{:S(2)}) async-start(bf16[1,128,1,5]{3,2,0,1:T(2,128)(2,1)} %copy.78), calls=%async_computation | async-start | bytes 131072 | tf_op jit(solution)/shard_map/all_to_all | solution.py:66
  23.8 0.8 select_reduce_fusion
  24.6 1.0 maximum_bitcast_fusion
  25.6 1.1 copy.82
  26.7 10.0 %all-to-all-done = bf16[1,128,1,5]{3,2,0,1:T(2,128)(2,1)S(1)} async-done(((bf16[1,128,1,5]{3,2,0,1:T(2,128)(2,1)}), bf16[1,128,1,5]{3,2,0,1:T(2,128)(2,1)S(1)}, u32[]{:S(2)}, u32[]{:S(2)}) %all-to-all-start) | async-done | bytes 1312 | tf_op jit(solution)/shard_map/all_to_all | solution.py:66
  36.8 6.2 %all-to-all-start.2 = ((bf16[2,128,1,640]{3,0,2,1:T(2,128)(2,1)}), bf16[2,128,1,640]{3,0,2,1:T(2,128)(2,1)S(1)}, u32[]{:S(2)}, u32[]{:S(2)}) async-start(bf16[2,128,1,640]{3,0,2,1:T(2,128)(2,1)} %copy.82), calls=%async_computation.2 | async-start | bytes 655360 | tf_op jit(solution)/shard_map/all_to_all | solution.py:65
  43.0 0.1 fusion.15
  43.1 0.7 gather_fusion
  43.8 0.1 bitcast_select_fusion.1
  43.9 0.7 copy.81
  44.6 13.1 %all-to-all-done.2 = bf16[2,128,1,640]{3,0,2,1:T(2,128)(2,1)S(1)} async-done(((bf16[2,128,1,640]{3,0,2,1:T(2,128)(2,1)}), bf16[2,128,1,640]{3,0,2,1:T(2,128)(2,1)S(1)}, u32[]{:S(2)}, u32[]{:S(2)}) %all-to-all-start.2) | async-done | bytes 327712 | tf_op jit(solution)/shard_map/all_to_all | solution.py:65
  57.7 8.6 %all-to-all-start.1 = ((bf16[1,128,1,5]{3,2,0,1:T(2,128)(2,1)}), bf16[1,128,1,5]{3,2,0,1:T(2,128)(2,1)S(1)}, u32[]{:S(2)}, u32[]{:S(2)}) async-start(bf16[1,128,1,5]{3,2,0,1:T(2,128)(2,1)} %copy.81), calls=%async_computation.1 | async-start | bytes 131072 | tf_op jit(solution)/shard_map/all_to_all | solution.py:72
  66.3 1.3 gather_fusion.1
  67.5 1.1 fusion.11
  68.7 10.5 %all-to-all-done.1 = bf16[1,128,1,5]{3,2,0,1:T(2,128)(2,1)S(1)} async-done(((bf16[1,128,1,5]{3,2,0,1:T(2,128)(2,1)}), bf16[1,128,1,5]{3,2,0,1:T(2,128)(2,1)S(1)}, u32[]{:S(2)}, u32[]{:S(2)}) %all-to-all-start.1) | async-done | bytes 1312 | tf_op jit(solution)/shard_map/all_to_all | solution.py:72
  79.2 6.4 %all-to-all-start.3 = ((bf16[2,128,1,640]{3,0,2,1:T(2,128)(2,1)}), bf16[2,128,1,640]{3,0,2,1:T(2,128)(2,1)S(1)}, u32[]{:S(2)}, u32[]{:S(2)}) async-start(bf16[2,128,1,640]{3,0,2,1:T(2,128)(2,1)} %fusion.11), calls=%async_computation.3 | async-start | bytes 655360 | tf_op jit(solution)/shard_map/all_to_all | solution.py:69
  85.6 0.3 copy.105
  85.8 0.3 copy.107
  86.1 0.1 convert_element_type.48
  86.2 0.1 slice_reduce_fusion
  86.3 0.1 slice_compare_fusion
  86.4 0.2 broadcast_in_dim.83
  86.6 0.1 bitcast_and_fusion
  86.7 13.5 %all-to-all-done.3 = bf16[2,128,1,640]{3,0,2,1:T(2,128)(2,1)S(1)} async-done(((bf16[2,128,1,640]{3,0,2,1:T(2,128)(2,1)}), bf16[2,128,1,640]{3,0,2,1:T(2,128)(2,1)S(1)}, u32[]{:S(2)}, u32[]{:S(2)}) %all-to-all-start.3) | async-done | bytes 327712 | tf_op jit(solution)/shard_map/all_to_all | solution.py:69
  100.2 0.5 fusion.16
  100.6 0.2 copy.104
  100.9 0.2 copy.106
  101.1 0.5 fusion.17
  101.6 0.1 broadcast_maximum_fusion
  101.7 0.4 fusion.8
  102.1 0.1 exponential_add_fusion
  102.2 0.6 fusion.6
  102.8 1.5 fusion.2
  104.3 0.3 fusion.5
  104.7 0.2 copy.92
  104.9 0.6 broadcast.200
  105.5 1.6 reduce.2
  107.1 0.9 reshape.298
  107.9 8.0 %all-to-all-start.4 = ((bf16[128,2,320]{2,1,0:T(2,128)(2,1)}), bf16[128,2,320]{2,1,0:T(2,128)(2,1)S(1)}, u32[]{:S(2)}, u32[]{:S(2)}) async-start(bf16[128,2,320]{2,1,0:T(2,128)(2,1)} %reshape.298), calls=%async_computation.4 | async-start | bytes 393216 | tf_op jit(solution)/shard_map/all_to_all | solution.py:88
  115.9 1.4 convolution_convert_fusion
  117.4 12.5 %all-to-all-done.4 = bf16[128,2,320]{2,1,0:T(2,128)(2,1)S(1)} async-done(((bf16[128,2,320]{2,1,0:T(2,128)(2,1)}), bf16[128,2,320]{2,1,0:T(2,128)(2,1)S(1)}, u32[]{:S(2)}, u32[]{:S(2)}) %all-to-all-start.4) | async-done | bytes 163872 | tf_op jit(solution)/shard_map/all_to_all | solution.py:88
  129.9 0.3 reshape.299
  130.2 0.9 gather_fusion.2
  131.1 0.1 bitcast_select_fusion
  131.2 0.3 copy.117
  131.4 1.6 reduce.3
  133.1 0.9 reshape.300
  133.9 7.4 %all-to-all-start.5 = ((bf16[128,2,320]{2,1,0:T(2,128)(2,1)}), bf16[128,2,320]{2,1,0:T(2,128)(2,1)}, u32[]{:S(2)}, u32[]{:S(2)}) async-start(bf16[128,2,320]{2,1,0:T(2,128)(2,1)} %reshape.300), calls=%async_computation.5 | async-start | bytes 393216 | tf_op jit(solution)/shard_map/all_to_all | solution.py:95
  141.3 0.3 fusion.3
  141.7 1.1 copy.95
  142.8 1.1 copy.94
  144.0 4.0 %pad_maximum_fusion = bf16[2,512,640]{2,0,1:T(2,128)(2,1)} fusion(bf16[1,512,640]{2,0,1:T(2,128)(2,1)S(1)} %copy.95, bf16[1,512,640]{2,0,1:T(2,128)(2,1)S(1)} %copy.94), kind=kLoop, calls=%fused_computation.11 | loop fusion | flops 2621440 | bytes 2621440 | tf_op jit(solution)/shard_map/stack | solution.py:47
  148.0 6.6 %all-to-all-done.5 = bf16[128,2,320]{2,1,0:T(2,128)(2,1)} async-done(((bf16[128,2,320]{2,1,0:T(2,128)(2,1)}), bf16[128,2,320]{2,1,0:T(2,128)(2,1)}, u32[]{:S(2)}, u32[]{:S(2)}) %all-to-all-start.5) | async-done | bytes 163872 | tf_op jit(solution)/shard_map/all_to_all | solution.py:95
  154.6 8.3 %all-to-all-start.6 = ((bf16[2,512,640]{2,0,1:T(2,128)(2,1)}), bf16[2,512,640]{2,0,1:T(2,128)(2,1)S(1)}, u32[]{:S(2)}, u32[]{:S(2)}) async-start(bf16[2,512,640]{2,0,1:T(2,128)(2,1)} %pad_maximum_fusion), calls=%async_computation.6 | async-start | bytes 2621440 | tf_op jit(solution)/shard_map/all_to_all | solution.py:98
  162.9 1.6 reshape.301
  164.6 0.7 copy.114
  165.3 14.1 %all-to-all-done.6 = bf16[2,512,640]{2,0,1:T(2,128)(2,1)S(1)} async-done(((bf16[2,512,640]{2,0,1:T(2,128)(2,1)}), bf16[2,512,640]{2,0,1:T(2,128)(2,1)S(1)}, u32[]{:S(2)}, u32[]{:S(2)}) %all-to-all-start.6) | async-done | bytes 1310752 | tf_op jit(solution)/shard_map/all_to_all | solution.py:98
  179.3 1.0 copy.96
  180.4 1.4 all_to_all.40
  (22 shorter events, 0.1 us)
Async XLA Ops:
  0.6 42.3 %copy-start.6 = (s32[128]{0:T(128)S(1)}, s32[128]{0:T(128)}, u32[]{:S(2)}) copy-start(s32[128]{0:T(128)} %param.12) | copy-start | bytes 1540
  0.6 42.3 %copy-start = (bf16[2,512,640]{2,1,0:T(8,128)(2,1)S(1)}, bf16[2,512,640]{2,1,0:T(8,128)(2,1)}, u32[]{:S(2)}) copy-start(bf16[2,512,640]{2,1,0:T(8,128)(2,1)} %param.10) | copy-start | bytes 3932164
  3.0 33.8 %all-to-all-start = ((bf16[1,128,1,5]{3,2,0,1:T(2,128)(2,1)}), bf16[1,128,1,5]{3,2,0,1:T(2,128)(2,1)S(1)}, u32[]{:S(2)}, u32[]{:S(2)}) async-start(bf16[1,128,1,5]{3,2,0,1:T(2,128)(2,1)} %copy.78), calls=%async_computation | async-start | bytes 131072 | tf_op jit(solution)/shard_map/all_to_all | solution.py:66
  36.8 20.9 %all-to-all-start.2 = ((bf16[2,128,1,640]{3,0,2,1:T(2,128)(2,1)}), bf16[2,128,1,640]{3,0,2,1:T(2,128)(2,1)S(1)}, u32[]{:S(2)}, u32[]{:S(2)}) async-start(bf16[2,128,1,640]{3,0,2,1:T(2,128)(2,1)} %copy.82), calls=%async_computation.2 | async-start | bytes 655360 | tf_op jit(solution)/shard_map/all_to_all | solution.py:65
  57.7 21.5 %all-to-all-start.1 = ((bf16[1,128,1,5]{3,2,0,1:T(2,128)(2,1)}), bf16[1,128,1,5]{3,2,0,1:T(2,128)(2,1)S(1)}, u32[]{:S(2)}, u32[]{:S(2)}) async-start(bf16[1,128,1,5]{3,2,0,1:T(2,128)(2,1)} %copy.81), calls=%async_computation.1 | async-start | bytes 131072 | tf_op jit(solution)/shard_map/all_to_all | solution.py:72
  79.2 21.0 %all-to-all-start.3 = ((bf16[2,128,1,640]{3,0,2,1:T(2,128)(2,1)}), bf16[2,128,1,640]{3,0,2,1:T(2,128)(2,1)S(1)}, u32[]{:S(2)}, u32[]{:S(2)}) async-start(bf16[2,128,1,640]{3,0,2,1:T(2,128)(2,1)} %fusion.11), calls=%async_computation.3 | async-start | bytes 655360 | tf_op jit(solution)/shard_map/all_to_all | solution.py:69
  85.6 1.0 copy-start.4
  100.9 0.7 copy-start.5
  101.1 1.1 copy-start.2
  104.3 11.6 %copy-start.3 = (bf16[1,128,1,640]{1,3,2,0:T(8,128)(2,1)S(1)}, bf16[1,128,1,640]{1,3,2,0:T(8,128)(2,1)}, u32[]{:S(2)}) copy-start(bf16[1,128,1,640]{1,3,2,0:T(8,128)(2,1)} %copy-done.2) | copy-start | bytes 491524
  107.9 21.9 %all-to-all-start.4 = ((bf16[128,2,320]{2,1,0:T(2,128)(2,1)}), bf16[128,2,320]{2,1,0:T(2,128)(2,1)S(1)}, u32[]{:S(2)}, u32[]{:S(2)}) async-start(bf16[128,2,320]{2,1,0:T(2,128)(2,1)} %reshape.298), calls=%async_computation.4 | async-start | bytes 393216 | tf_op jit(solution)/shard_map/all_to_all | solution.py:88
  131.4 10.2 %copy-start.1 = (bf16[5,128,512]{2,1,0:T(8,128)(2,1)S(1)}, bf16[5,128,512]{2,1,0:T(8,128)(2,1)}, u32[]{:S(2)}) copy-start(bf16[5,128,512]{2,1,0:T(8,128)(2,1)} %convolution_convert_fusion) | copy-start | bytes 1966084
  133.9 20.7 %all-to-all-start.5 = ((bf16[128,2,320]{2,1,0:T(2,128)(2,1)}), bf16[128,2,320]{2,1,0:T(2,128)(2,1)}, u32[]{:S(2)}, u32[]{:S(2)}) async-start(bf16[128,2,320]{2,1,0:T(2,128)(2,1)} %reshape.300), calls=%async_computation.5 | async-start | bytes 393216 | tf_op jit(solution)/shard_map/all_to_all | solution.py:95
  154.6 24.7 %all-to-all-start.6 = ((bf16[2,512,640]{2,0,1:T(2,128)(2,1)}), bf16[2,512,640]{2,0,1:T(2,128)(2,1)S(1)}, u32[]{:S(2)}, u32[]{:S(2)}) async-start(bf16[2,512,640]{2,0,1:T(2,128)(2,1)} %pad_maximum_fusion), calls=%async_computation.6 | async-start | bytes 2621440 | tf_op jit(solution)/shard_map/all_to_all | solution.py:98
where the time goes:
time: 182 us
  waiting for transfers between devices  80.3 us (44%)
  starting transfers between devices  65.6 us (36%)
  local copies, waits for them, and re-layouts  17.5 us (10%)
  other arithmetic  12.7 us (7%)
  matrix products  4.67 us (3%)
    all_to_all x1, starting transfers between devices, shards(): lax.all_to_all(text_tags, 'ctx', split_axis=1, concat_axis=1, tiled=True)  20.8 us
    all_to_all x1, waiting for transfers between devices, shards(): lax.all_to_all(home_adjoint, 'head', split_axis=1, concat_axis=2, tiled=T...  14.1 us
    all_to_all x1, waiting for transfers between devices, shards(): lax.all_to_all(jnp.take(first_text, inverse, axis=1), 'ctx', split_axis=1...  13.5 us
    all_to_all x1, waiting for transfers between devices, shards(): lax.all_to_all(stacked, 'ctx', split_axis=1, concat_axis=1, tiled=True)  13.1 us
    all_to_all x1, waiting for transfers between devices, shards(): lax.all_to_all(grad_visit.reshape(1, owners, text_rows // owners, feature...  12.5 us
    all_to_all x1, waiting for transfers between devices, shards(): lax.all_to_all(jnp.take(first_tags, inverse, axis=1), 'ctx', split_axis=1...  10.5 us
    all_to_all x1, waiting for transfers between devices, shards(): lax.all_to_all(text_tags, 'ctx', split_axis=1, concat_axis=1, tiled=True)  10 us
    all_to_all x1, starting transfers between devices, shards(): lax.all_to_all(jnp.take(first_tags, inverse, axis=1), 'ctx', split_axis=1...  8.58 us
  transfers between devices with their start and end apart: 7, of which 7 were waited for; matrix products, arithmetic and copies ran while one was open for 10% of the time, Pallas kernels for 0%

commit v1 on v0

--- a/solution.py
+++ b/solution.py
@@ -95,7 +95,12 @@
     grad_query = lax.all_to_all(
         jnp.take(returning, pairing, axis=1), "ctx", split_axis=1, concat_axis=1, tiled=True
     ).reshape(text_rows, feature_width)
-    grad_kv = lax.all_to_all(home_adjoint, "head", split_axis=1, concat_axis=2, tiled=True)
+    grad_kv = jnp.concatenate(
+        lax.all_to_all(
+            jnp.stack(jnp.split(home_adjoint, lax.axis_size("head"), axis=1)), "head", 0, 0
+        ),
+        axis=2,
+    )
     return (grad_query, grad_kv)
 
 

time: 182 us -> 182 us (level)
  waiting for transfers between devices: 80.3 us -> 87.1 us
  other arithmetic: 12.7 us -> 10.2 us
  local copies, waits for them, and re-layouts: 17.5 us -> 15 us
    all_to_all x1, waiting for transfers between devices: 6.64 us -> 12.1 us  [shards(): lax.all_to_all(jnp.take(returning, pairing, axis=1), 'ctx', split_axis=1,...]
    reshape x0 -> x2, local copies, waits for them, and re-layouts: none -> 2.95 us  [shards(): jnp.concatenate(lax.all_to_all(jnp.stack(jnp.split(home_adjoint, lax.axis...]
    another operation x2 -> x3, other arithmetic: 4.79 us -> 2.12 us  [the longest x2 1.46 us: shards(): jnp.stack(jnp.split(home_adjoint, lax.axis_size('head'), axis=1))]
    all_to_all x2 -> x0, local copies, waits for them, and re-layouts: 2.38 us -> none  [shards(): lax.all_to_all(home_adjoint, 'head', split_axis=1, concat_axis=2, tiled=T...]
    another operation x2 -> x0, local copies, waits for them, and re-layouts: 2.29 us -> none  [attend(): jnp.stack([grad_keys.reshape(frame_rows, -1), grad_values.reshape(frame_r...]
  transfers between devices with their start and end apart: 7 -> 7, of which waited for: 7 -> 7; matrix products, arithmetic and copies ran while one was open for 10% -> 7% of each run, Pallas kernels for 0% -> 0%
where the time goes in v1:
time: 182 us; the launch traced here: 181 us
  waiting for transfers between devices  87.1 us (48%)
  starting transfers between devices  64.4 us (35%)
  local copies, waits for them, and re-layouts  15 us (8%)
  other arithmetic  10.2 us (6%)
  matrix products  3.78 us (2%)
    all_to_all x1, starting transfers between devices, shards(): lax.all_to_all(text_tags, 'ctx', split_axis=1, concat_axis=1, tiled=True)  20.8 us
    all_to_all x1, waiting for transfers between devices, shards(): lax.all_to_all(jnp.stack(jnp.split(home_adjoint, lax.axis_size('head'), a...  15.4 us
    all_to_all x1, waiting for transfers between devices, shards(): lax.all_to_all(jnp.take(first_text, inverse, axis=1), 'ctx', split_axis=1...  13.5 us
    all_to_all x1, waiting for transfers between devices, shards(): lax.all_to_all(stacked, 'ctx', split_axis=1, concat_axis=1, tiled=True)  13.1 us
    all_to_all x1, waiting for transfers between devices, shards(): lax.all_to_all(grad_visit.reshape(1, owners, text_rows // owners, feature...  12.5 us
    all_to_all x1, waiting for transfers between devices, shards(): lax.all_to_all(jnp.take(returning, pairing, axis=1), 'ctx', split_axis=1,...  12.1 us
    all_to_all x1, waiting for transfers between devices, shards(): lax.all_to_all(jnp.take(first_tags, inverse, axis=1), 'ctx', split_axis=1...  10.5 us
    all_to_all x1, waiting for transfers between devices, shards(): lax.all_to_all(text_tags, 'ctx', split_axis=1, concat_axis=1, tiled=True)  10 us
  transfers between devices with their start and end apart: 7, of which 7 were waited for; matrix products, arithmetic and copies ran while one was open for 7% of the time, Pallas kernels for 0%

profile of v1, /device:TPU:1, one launch (start us, length us, event | category | flops | bytes accessed | tf_op | source)
XLA Modules:
  0.0 181.4 jit_solution(14637316252824624414)
XLA Ops:
  0.7 0.8 convert_bitcast_fusion.1
  1.4 0.7 convert_bitcast_fusion
  2.1 0.1 pad.9.clone
  2.2 0.1 pad_maximum_fusion.2
  2.2 0.8 copy.74
  3.0 20.8 %all-to-all-start = ((bf16[1,128,1,5]{3,2,0,1:T(2,128)(2,1)}), bf16[1,128,1,5]{3,2,0,1:T(2,128)(2,1)S(1)}, u32[]{:S(2)}, u32[]{:S(2)}) async-start(bf16[1,128,1,5]{3,2,0,1:T(2,128)(2,1)} %copy.74), calls=%async_computation | async-start | bytes 131072 | tf_op jit(solution)/shard_map/all_to_all | solution.py:66
  23.8 0.8 select_reduce_fusion
  24.6 1.0 maximum_bitcast_fusion
  25.6 1.1 copy.78
  26.7 10.0 %all-to-all-done = bf16[1,128,1,5]{3,2,0,1:T(2,128)(2,1)S(1)} async-done(((bf16[1,128,1,5]{3,2,0,1:T(2,128)(2,1)}), bf16[1,128,1,5]{3,2,0,1:T(2,128)(2,1)S(1)}, u32[]{:S(2)}, u32[]{:S(2)}) %all-to-all-start) | async-done | bytes 1312 | tf_op jit(solution)/shard_map/all_to_all | solution.py:66
  36.8 6.2 %all-to-all-start.2 = ((bf16[2,128,1,640]{3,0,2,1:T(2,128)(2,1)}), bf16[2,128,1,640]{3,0,2,1:T(2,128)(2,1)S(1)}, u32[]{:S(2)}, u32[]{:S(2)}) async-start(bf16[2,128,1,640]{3,0,2,1:T(2,128)(2,1)} %copy.78), calls=%async_computation.2 | async-start | bytes 655360 | tf_op jit(solution)/shard_map/all_to_all | solution.py:65
  43.0 0.1 fusion.22
  43.1 0.7 gather_fusion
  43.8 0.1 bitcast_select_fusion.1
  43.9 0.7 copy.77
  44.6 13.1 %all-to-all-done.2 = bf16[2,128,1,640]{3,0,2,1:T(2,128)(2,1)S(1)} async-done(((bf16[2,128,1,640]{3,0,2,1:T(2,128)(2,1)}), bf16[2,128,1,640]{3,0,2,1:T(2,128)(2,1)S(1)}, u32[]{:S(2)}, u32[]{:S(2)}) %all-to-all-start.2) | async-done | bytes 327712 | tf_op jit(solution)/shard_map/all_to_all | solution.py:65
  57.7 8.6 %all-to-all-start.1 = ((bf16[1,128,1,5]{3,2,0,1:T(2,128)(2,1)}), bf16[1,128,1,5]{3,2,0,1:T(2,128)(2,1)S(1)}, u32[]{:S(2)}, u32[]{:S(2)}) async-start(bf16[1,128,1,5]{3,2,0,1:T(2,128)(2,1)} %copy.77), calls=%async_computation.1 | async-start | bytes 131072 | tf_op jit(solution)/shard_map/all_to_all | solution.py:72
  66.3 1.3 gather_fusion.1
  67.5 1.1 fusion.18
  68.7 10.5 %all-to-all-done.1 = bf16[1,128,1,5]{3,2,0,1:T(2,128)(2,1)S(1)} async-done(((bf16[1,128,1,5]{3,2,0,1:T(2,128)(2,1)}), bf16[1,128,1,5]{3,2,0,1:T(2,128)(2,1)S(1)}, u32[]{:S(2)}, u32[]{:S(2)}) %all-to-all-start.1) | async-done | bytes 1312 | tf_op jit(solution)/shard_map/all_to_all | solution.py:72
  79.2 6.4 %all-to-all-start.3 = ((bf16[2,128,1,640]{3,0,2,1:T(2,128)(2,1)}), bf16[2,128,1,640]{3,0,2,1:T(2,128)(2,1)S(1)}, u32[]{:S(2)}, u32[]{:S(2)}) async-start(bf16[2,128,1,640]{3,0,2,1:T(2,128)(2,1)} %fusion.18), calls=%async_computation.3 | async-start | bytes 655360 | tf_op jit(solution)/shard_map/all_to_all | solution.py:69
  85.6 0.3 copy.101
  85.8 0.3 copy.99
  86.1 0.1 convert_element_type.48
  86.2 0.1 slice_reduce_fusion
  86.3 0.1 slice_compare_fusion
  86.4 0.2 broadcast_in_dim.83
  86.6 0.1 bitcast_and_fusion
  86.7 13.5 %all-to-all-done.3 = bf16[2,128,1,640]{3,0,2,1:T(2,128)(2,1)S(1)} async-done(((bf16[2,128,1,640]{3,0,2,1:T(2,128)(2,1)}), bf16[2,128,1,640]{3,0,2,1:T(2,128)(2,1)S(1)}, u32[]{:S(2)}, u32[]{:S(2)}) %all-to-all-start.3) | async-done | bytes 327712 | tf_op jit(solution)/shard_map/all_to_all | solution.py:69
  100.2 0.5 fusion.23
  100.6 0.9 copy.100
  101.5 0.2 copy.98
  101.8 0.5 fusion.24
  102.2 0.1 broadcast_maximum_fusion
  102.3 0.4 fusion.8
  102.7 0.1 exponential_add_fusion
  102.8 0.6 fusion.6
  103.4 0.6 fusion.2
  104.1 0.3 fusion.5
  104.4 0.2 copy.88
  104.6 0.5 broadcast.200
  105.2 1.6 reduce.2
  106.8 0.9 reshape.306
  107.6 8.0 %all-to-all-start.4 = ((bf16[128,2,320]{2,1,0:T(2,128)(2,1)}), bf16[128,2,320]{2,1,0:T(2,128)(2,1)S(1)}, u32[]{:S(2)}, u32[]{:S(2)}) async-start(bf16[128,2,320]{2,1,0:T(2,128)(2,1)} %reshape.306), calls=%async_computation.4 | async-start | bytes 393216 | tf_op jit(solution)/shard_map/all_to_all | solution.py:88
  115.6 1.4 convolution_convert_fusion
  117.1 12.5 %all-to-all-done.4 = bf16[128,2,320]{2,1,0:T(2,128)(2,1)S(1)} async-done(((bf16[128,2,320]{2,1,0:T(2,128)(2,1)}), bf16[128,2,320]{2,1,0:T(2,128)(2,1)S(1)}, u32[]{:S(2)}, u32[]{:S(2)}) %all-to-all-start.4) | async-done | bytes 163872 | tf_op jit(solution)/shard_map/all_to_all | solution.py:88
  129.6 0.3 reshape.307
  129.9 0.9 gather_fusion.2
  130.8 0.1 bitcast_select_fusion
  130.9 0.3 copy.111
  131.1 0.0 copy-start.1
  131.1 1.7 reduce.3
  132.8 0.9 reshape.308
  133.7 6.2 %all-to-all-start.5 = ((bf16[128,2,320]{2,1,0:T(2,128)(2,1)}), bf16[128,2,320]{2,1,0:T(2,128)(2,1)S(1)}, u32[]{:S(2)}, u32[]{:S(2)}) async-start(bf16[128,2,320]{2,1,0:T(2,128)(2,1)} %reshape.308), calls=%async_computation.5 | async-start | bytes 393216 | tf_op jit(solution)/shard_map/all_to_all | solution.py:95
  139.8 0.3 fusion.3
  140.2 0.2 fusion.12
  140.4 1.2 pad_maximum_fusion
  141.6 12.1 %all-to-all-done.5 = bf16[128,2,320]{2,1,0:T(2,128)(2,1)S(1)} async-done(((bf16[128,2,320]{2,1,0:T(2,128)(2,1)}), bf16[128,2,320]{2,1,0:T(2,128)(2,1)S(1)}, u32[]{:S(2)}, u32[]{:S(2)}) %all-to-all-start.5) | async-done | bytes 163872 | tf_op jit(solution)/shard_map/all_to_all | solution.py:95
  153.7 8.4 %all-to-all-start.6 = ((bf16[4,2,128,640]{2,3,1,0:T(8,128)(2,1)}), bf16[4,2,128,640]{2,3,1,0:T(8,128)(2,1)S(1)}, u32[]{:S(2)}, u32[]{:S(2)}) async-start(bf16[4,2,128,640]{2,3,1,0:T(8,128)(2,1)} %pad_maximum_fusion), calls=%async_computation.6 | async-start | bytes 2621440 | tf_op jit(solution)/shard_map/all_to_all | solution.py:99
  162.1 0.3 reshape.309
  162.4 0.7 copy.108
  163.0 15.4 %all-to-all-done.6 = bf16[4,2,128,640]{2,3,1,0:T(8,128)(2,1)S(1)} async-done(((bf16[4,2,128,640]{2,3,1,0:T(8,128)(2,1)}), bf16[4,2,128,640]{2,3,1,0:T(8,128)(2,1)S(1)}, u32[]{:S(2)}, u32[]{:S(2)}) %all-to-all-start.6) | async-done | bytes 1310752 | tf_op jit(solution)/shard_map/all_to_all | solution.py:99
  178.5 1.6 copy.90
  180.1 1.4 reshape.262
  (21 shorter events, 0.1 us)
Async XLA Ops:
  0.6 42.3 %copy-start.6 = (s32[128]{0:T(128)S(1)}, s32[128]{0:T(128)}, u32[]{:S(2)}) copy-start(s32[128]{0:T(128)} %param.12) | copy-start | bytes 1540
  0.6 42.3 %copy-start = (bf16[2,512,640]{2,1,0:T(8,128)(2,1)S(1)}, bf16[2,512,640]{2,1,0:T(8,128)(2,1)}, u32[]{:S(2)}) copy-start(bf16[2,512,640]{2,1,0:T(8,128)(2,1)} %param.10) | copy-start | bytes 3932164
  3.0 33.8 %all-to-all-start = ((bf16[1,128,1,5]{3,2,0,1:T(2,128)(2,1)}), bf16[1,128,1,5]{3,2,0,1:T(2,128)(2,1)S(1)}, u32[]{:S(2)}, u32[]{:S(2)}) async-start(bf16[1,128,1,5]{3,2,0,1:T(2,128)(2,1)} %copy.74), calls=%async_computation | async-start | bytes 131072 | tf_op jit(solution)/shard_map/all_to_all | solution.py:66
  36.8 20.9 %all-to-all-start.2 = ((bf16[2,128,1,640]{3,0,2,1:T(2,128)(2,1)}), bf16[2,128,1,640]{3,0,2,1:T(2,128)(2,1)S(1)}, u32[]{:S(2)}, u32[]{:S(2)}) async-start(bf16[2,128,1,640]{3,0,2,1:T(2,128)(2,1)} %copy.78), calls=%async_computation.2 | async-start | bytes 655360 | tf_op jit(solution)/shard_map/all_to_all | solution.py:65
  57.7 21.5 %all-to-all-start.1 = ((bf16[1,128,1,5]{3,2,0,1:T(2,128)(2,1)}), bf16[1,128,1,5]{3,2,0,1:T(2,128)(2,1)S(1)}, u32[]{:S(2)}, u32[]{:S(2)}) async-start(bf16[1,128,1,5]{3,2,0,1:T(2,128)(2,1)} %copy.77), calls=%async_computation.1 | async-start | bytes 131072 | tf_op jit(solution)/shard_map/all_to_all | solution.py:72
  79.2 21.0 %all-to-all-start.3 = ((bf16[2,128,1,640]{3,0,2,1:T(2,128)(2,1)}), bf16[2,128,1,640]{3,0,2,1:T(2,128)(2,1)S(1)}, u32[]{:S(2)}, u32[]{:S(2)}) async-start(bf16[2,128,1,640]{3,0,2,1:T(2,128)(2,1)} %fusion.18), calls=%async_computation.3 | async-start | bytes 655360 | tf_op jit(solution)/shard_map/all_to_all | solution.py:69
  85.6 1.0 copy-start.4
  101.5 0.7 copy-start.5
  101.7 1.1 copy-start.2
  104.0 11.6 %copy-start.3 = (bf16[1,128,1,640]{1,3,2,0:T(8,128)(2,1)S(1)}, bf16[1,128,1,640]{1,3,2,0:T(8,128)(2,1)}, u32[]{:S(2)}) copy-start(bf16[1,128,1,640]{1,3,2,0:T(8,128)(2,1)} %copy.100) | copy-start | bytes 491524
  107.6 21.9 %all-to-all-start.4 = ((bf16[128,2,320]{2,1,0:T(2,128)(2,1)}), bf16[128,2,320]{2,1,0:T(2,128)(2,1)S(1)}, u32[]{:S(2)}, u32[]{:S(2)}) async-start(bf16[128,2,320]{2,1,0:T(2,128)(2,1)} %reshape.306), calls=%async_computation.4 | async-start | bytes 393216 | tf_op jit(solution)/shard_map/all_to_all | solution.py:88
  131.1 9.0 %copy-start.1 = (bf16[5,128,512]{2,1,0:T(8,128)(2,1)S(1)}, bf16[5,128,512]{2,1,0:T(8,128)(2,1)}, u32[]{:S(2)}) copy-start(bf16[5,128,512]{2,1,0:T(8,128)(2,1)} %convolution_convert_fusion) | copy-start | bytes 1966084
  133.7 20.1 %all-to-all-start.5 = ((bf16[128,2,320]{2,1,0:T(2,128)(2,1)}), bf16[128,2,320]{2,1,0:T(2,128)(2,1)S(1)}, u32[]{:S(2)}, u32[]{:S(2)}) async-start(bf16[128,2,320]{2,1,0:T(2,128)(2,1)} %reshape.308), calls=%async_computation.5 | async-start | bytes 393216 | tf_op jit(solution)/shard_map/all_to_all | solution.py:95
  153.7 24.8 %all-to-all-start.6 = ((bf16[4,2,128,640]{2,3,1,0:T(8,128)(2,1)}), bf16[4,2,128,640]{2,3,1,0:T(8,128)(2,1)S(1)}, u32[]{:S(2)}, u32[]{:S(2)}) async-start(bf16[4,2,128,640]{2,3,1,0:T(8,128)(2,1)} %pad_maximum_fusion), calls=%async_computation.6 | async-start | bytes 2621440 | tf_op jit(solution)/shard_map/all_to_all | solution.py:99
